TPU v7x, 32 devices: a whole 2x2x4 slice. The times are simulated.
32 devices in a mesh: dp: 8 (over z, y), tensor: 4 (over x, core).
Axes of the slice: x: 2, y: 2, z: 4, core: 2. Of those that a mesh axis runs over, the one named last changes fastest.
Arguments:
- tokens: bfloat16 [8, 512, 768], P('dp'), may hold values from -6 to 6
- cotangent: bfloat16 [8, 512, 768], P('dp'), may hold values from -6 to 6
- norm_gain: float32 [768], replicated, may hold values from 0.1 to 1.9
- w_z: bfloat16 [768, 1536], P(None, 'tensor'), may hold values from -0.21875 to 0.21875
- w_x: bfloat16 [768, 1536], P(None, 'tensor'), may hold values from -0.21875 to 0.21875
- w_bc: bfloat16 [768, 256], replicated, may hold values from -0.21875 to 0.21875
- w_dt: bfloat16 [768, 24], P(None, 'tensor'), may hold values from -0.21875 to 0.21875
- conv_x: float32 [4, 1536], P(None, 'tensor'), may hold values from -3 to 3
- conv_x_bias: float32 [1536], P('tensor'), may hold values from -3 to 3
- conv_bc: float32 [4, 256], replicated, may hold values from -3 to 3
- conv_bc_bias: float32 [256], replicated, may hold values from -3 to 3
- dt_bias: float32 [24], P('tensor'), may hold values from -5 to -1
- a_log: float32 [24], P('tensor'), may hold values from -4 to 2
- d_skip: float32 [24], P('tensor'), may hold values from 0.5 to 2
- gate_gain: float32 [1536], P('tensor'), may hold values from 0.1 to 1.9
- w_out: bfloat16 [1536, 768], P('tensor'), may hold values from -0.15625 to 0.15625
Outputs:
- result: bfloat16 [8, 512, 768], P('dp')
- grad_x: bfloat16 [8, 512, 768], P('dp')
- grad_norm_gain: float32 [768], replicated
- grad_w_z: float32 [768, 1536], P(None, 'tensor')
- grad_w_x: float32 [768, 1536], P(None, 'tensor')
- grad_w_bc: float32 [768, 256], replicated
- grad_w_dt: float32 [768, 24], P(None, 'tensor')
- grad_conv_x: float32 [4, 1536], P(None, 'tensor')
- grad_conv_x_bias: float32 [1536], P('tensor')
- grad_conv_bc: float32 [4, 256], replicated
- grad_conv_bc_bias: float32 [256], replicated
- grad_dt_bias: float32 [24], P('tensor')
- grad_a_log: float32 [24], P('tensor')
- grad_d_skip: float32 [24], P('tensor')
- grad_gate_gain: float32 [1536], P('tensor')
- grad_w_out: float32 [1536, 768], P('tensor')
All inputs are finite; a program needn't handle non-finite values.
Results may differ from a plain program's by a relative error of at most 0.013.
Values may be sent and summed in bfloat16 or wider, within the bound.
A program may use at most 128 MiB of HBM per device.

v0:
```python
import jax
import jax.numpy as jnp
from jax import lax
from jax.sharding import PartitionSpec as P

Q = 256
epsilon = 1e-05
highest = lax.Precision.HIGHEST


def input_norm(values, norm_gain):
    return (
        values
        * lax.rsqrt(jnp.mean(values * values, axis=-1, keepdims=True) + epsilon)
        * norm_gain[None, :]
    )


def causal_conv(values, kernel, shift_bias):
    length = values.shape[0]
    kernel_taps = kernel.shape[0]
    padded = jnp.pad(values, ((kernel_taps - 1, 0), (0, 0)))
    summed = jnp.zeros_like(values) + shift_bias[None, :]
    for offset in range(kernel_taps):
        summed = summed + kernel[offset][None, :] * padded[offset : offset + length]
    return summed


def state_scan(xheads, b_rows, c_rows, step_size, log_decay):
    length, head_count, head_dim = xheads.shape
    blocks = length // Q
    states = b_rows.shape[1]
    causal_mask = jnp.arange(Q)[:, None] >= jnp.arange(Q)[None, :]

    def advance(carried_state, pieces):
        x_blk, b_blk, c_blk, dt_blk, a_blk = pieces
        cumulative = jnp.cumsum(a_blk, axis=0)
        spread = jnp.where(
            causal_mask[:, :, None], cumulative[:, None, :] - cumulative[None, :, :], -jnp.inf
        )
        scores = jnp.dot(c_blk, b_blk.T, precision=highest)
        mixing = scores[:, :, None] * jnp.exp(spread) * dt_blk[None, :, :]
        inside = jnp.einsum("tsh,shp->thp", mixing, x_blk, precision=highest)
        carried = (
            jnp.einsum("tn,hpn->thp", c_blk, carried_state, precision=highest)
            * jnp.exp(cumulative)[:, :, None]
        )
        weight_tail = jnp.exp(cumulative[-1][None, :] - cumulative) * dt_blk
        update = jnp.einsum(
            "shp,sn->hpn", x_blk * weight_tail[:, :, None], b_blk, precision=highest
        )
        carried_state = carried_state * jnp.exp(cumulative[-1])[:, None, None] + update
        return (carried_state, inside + carried)

    initial = jnp.zeros((head_count, head_dim, states), jnp.float32)
    pieces = (
        xheads.reshape(blocks, Q, head_count, head_dim),
        b_rows.reshape(blocks, Q, states),
        c_rows.reshape(blocks, Q, states),
        step_size.reshape(blocks, Q, head_count),
        log_decay.reshape(blocks, Q, head_count),
    )
    _, outputs = lax.scan(advance, initial, pieces)
    return outputs.reshape(length, head_count, head_dim)


def mixer(
    x_pre, bc_pre, dt_pre, conv_x, conv_x_bias, conv_bc, conv_bc_bias, dt_bias, a_log, d_skip
):
    length, head_count = dt_pre.shape
    xconv = jax.nn.silu(causal_conv(x_pre, conv_x, conv_x_bias))
    bcconv = jax.nn.silu(causal_conv(bc_pre, conv_bc, conv_bc_bias))
    states = bc_pre.shape[1] // 2
    step_size = jax.nn.softplus(dt_pre + dt_bias[None, :])
    log_decay = -step_size * jnp.exp(a_log)[None, :]
    xheads = xconv.reshape(length, head_count, -1)
    mixed = state_scan(xheads, bcconv[:, :states], bcconv[:, states:], step_size, log_decay)
    mixed = mixed + d_skip[None, :, None] * xheads
    return mixed.reshape(length, -1)


def batched_mixer(
    x_pre, bc_pre, dt_pre, conv_x, conv_x_bias, conv_bc, conv_bc_bias, dt_bias, a_log, d_skip
):
    mapped = jax.vmap(mixer, in_axes=(0, 0, 0, None, None, None, None, None, None, None))
    return mapped(
        x_pre, bc_pre, dt_pre, conv_x, conv_x_bias, conv_bc, conv_bc_bias, dt_bias, a_log, d_skip
    )


def silu_slope(values):
    sigmoid = jax.nn.sigmoid(values)
    return sigmoid * (1.0 + values * (1.0 - sigmoid))


def contract_rows(left, right):
    return lax.dot_general(
        left, right, (((0,), (0,)), ((), ())), preferred_element_type=jnp.float32
    )


def contract_cols(left, right):
    return lax.dot_general(
        left, right, (((1,), (1,)), ((), ())), preferred_element_type=jnp.float32
    )


def per_device(
    tokens,
    cotangent,
    norm_gain,
    w_z,
    w_x,
    w_bc,
    w_dt,
    conv_x,
    conv_x_bias,
    conv_bc,
    conv_bc_bias,
    dt_bias,
    a_log,
    d_skip,
    gate_gain,
    w_out,
):
    seq_count, length, width = tokens.shape
    row_count = seq_count * length
    share_rows = row_count // lax.axis_size("tensor")
    first_row = lax.axis_index("tensor") * share_rows
    widef = tokens.reshape(row_count, width).astype(jnp.float32)
    normed = input_norm(widef, norm_gain).astype(jnp.bfloat16)
    gate_pre = jnp.dot(normed, w_z, preferred_element_type=jnp.float32)
    x_pre = jnp.dot(normed, w_x, preferred_element_type=jnp.float32)
    bc_pre = jnp.dot(normed, w_bc, preferred_element_type=jnp.float32)
    dt_pre = jnp.dot(normed, w_dt, preferred_element_type=jnp.float32)
    mixed, mixer_back = jax.vjp(
        batched_mixer,
        x_pre.reshape(seq_count, length, -1),
        bc_pre.reshape(seq_count, length, -1),
        dt_pre.reshape(seq_count, length, -1),
        conv_x,
        conv_x_bias,
        conv_bc,
        conv_bc_bias,
        dt_bias,
        a_log,
        d_skip,
    )
    mixed = mixed.reshape(row_count, -1)
    inner_total = mixed.shape[1] * lax.axis_size("tensor")
    gate_act = jax.nn.silu(gate_pre)
    gated = mixed * gate_act
    squares = lax.psum(jnp.sum(gated * gated, axis=-1), "tensor")
    inverse = lax.rsqrt(squares / inner_total + epsilon)[:, None]
    gated_n = (gated * inverse * gate_gain[None, :]).astype(jnp.bfloat16)
    partial_out = jnp.dot(gated_n, w_out, preferred_element_type=jnp.float32)
    summed_out = lax.psum(partial_out.astype(jnp.bfloat16), "tensor").astype(jnp.float32)
    result = (widef + summed_out).astype(jnp.bfloat16)
    result = result.reshape(seq_count, length, width)
    cotan = cotangent.reshape(row_count, width)
    grad_w_out = contract_rows(gated_n, cotan)
    d_gated_n = contract_cols(cotan, w_out)
    grad_gate_gain = jnp.sum(d_gated_n * gated * inverse, axis=0)
    scaled = gate_gain[None, :] * d_gated_n
    products = lax.psum(jnp.sum(scaled * gated, axis=-1), "tensor")
    d_gated = inverse * scaled - gated * inverse**3 * (products / inner_total)[:, None]
    d_mixed = d_gated * gate_act
    d_gate_pre = d_gated * mixed * silu_slope(gate_pre)
    back = mixer_back(d_mixed.reshape(seq_count, length, -1))
    d_gate_b = d_gate_pre.astype(jnp.bfloat16)
    d_x_b = back[0].reshape(row_count, -1).astype(jnp.bfloat16)
    d_bc_b = back[1].reshape(row_count, -1).astype(jnp.bfloat16)
    d_dt_b = back[2].reshape(row_count, -1).astype(jnp.bfloat16)
    grad_w_z = contract_rows(normed, d_gate_b)
    grad_w_x = contract_rows(normed, d_x_b)
    grad_w_bc = contract_rows(normed, d_bc_b)
    grad_w_dt = contract_rows(normed, d_dt_b)
    d_normed_part = (
        contract_cols(d_gate_b, w_z)
        + contract_cols(d_x_b, w_x)
        + contract_cols(d_bc_b, w_bc)
        + contract_cols(d_dt_b, w_dt)
    )
    input_rows = lax.dynamic_slice_in_dim(widef, first_row, share_rows, 0)
    _, share_back = jax.vjp(input_norm, input_rows, norm_gain)
    d_normed = lax.psum(d_normed_part.astype(jnp.bfloat16), "tensor").astype(jnp.float32)
    _, full_back = jax.vjp(input_norm, widef, norm_gain)
    d_tokens, _ = full_back(d_normed)
    d_normed_rows = lax.dynamic_slice_in_dim(d_normed, first_row, share_rows, 0)
    _, grad_norm_gain = share_back(d_normed_rows)
    grad_x = (cotan.astype(jnp.float32) + d_tokens).astype(jnp.bfloat16)
    grad_x = grad_x.reshape(seq_count, length, width)
    grad_w_bc, grad_conv_bc, grad_conv_bc_bias, grad_norm_gain = lax.psum(
        (grad_w_bc, back[5], back[6], grad_norm_gain), ("dp", "tensor")
    )
    reduced = lax.psum(
        (
            grad_w_z,
            grad_w_x,
            grad_w_dt,
            back[3],
            back[4],
            back[7],
            back[8],
            back[9],
            grad_gate_gain,
            grad_w_out,
        ),
        "dp",
    )
    (
        grad_w_z,
        grad_w_x,
        grad_w_dt,
        grad_conv_x,
        grad_conv_x_bias,
        grad_dt_bias,
        grad_a_log,
        grad_d_skip,
        grad_gate_gain,
        grad_w_out,
    ) = reduced
    return (
        result,
        grad_x,
        grad_norm_gain,
        grad_w_z,
        grad_w_x,
        grad_w_bc,
        grad_w_dt,
        grad_conv_x,
        grad_conv_x_bias,
        grad_conv_bc,
        grad_conv_bc_bias,
        grad_dt_bias,
        grad_a_log,
        grad_d_skip,
        grad_gate_gain,
        grad_w_out,
    )


def solution(mesh):
    placed = (
        P("dp", None, None),
        P("dp", None, None),
        P(),
        P(None, "tensor"),
        P(None, "tensor"),
        P(),
        P(None, "tensor"),
        P(None, "tensor"),
        P("tensor"),
        P(),
        P(),
        P("tensor"),
        P("tensor"),
        P("tensor"),
        P("tensor"),
        P("tensor", None),
    )
    return jax.shard_map(
        per_device,
        mesh=mesh,
        in_specs=placed,
        out_specs=(
            P("dp", None, None),
            P("dp", None, None),
            P(),
            P(None, "tensor"),
            P(None, "tensor"),
            P(),
            P(None, "tensor"),
            P(None, "tensor"),
            P("tensor"),
            P(),
            P(),
            P("tensor"),
            P("tensor"),
            P("tensor"),
            P("tensor"),
            P("tensor", None),
        ),
        check_vma=False,
    )
```

profile of v0, /device:TPU:0, one launch (start us, length us, event | category | flops | bytes accessed | tf_op | source)
XLA Modules:
  0.0 580.4 jit_solution(8823095844115345862)
XLA Ops:
  23.5 54.7 %while.71 = (s32[]{:T(128)}, f32[1,6,64,128]{3,2,1,0:T(8,128)S(1)}, f32[2,1,256,6,64]{2,0,4,3,1:T(2,128)}, f32[2,1,128,256]{2,3,1,0:T(8,128)}, f32[2,1,256,256,6...) while((s32[]{:T(128)}, f32[1,6,64,128]{3,2,1,0:T(8,128)S(1)}, ...), condition=%wide.region_4.5_spmd.clone.clone, body=%wide.region_1.4_spmd.clone.clone.sunk | while | flops 708627456 | bytes 15328889 | solution.py:63
  28.7 2.6 multiply_dynamic-update-slice_fusion.4
  36.7 9.0 %dynamic_update_slice.218 = f32[2,1,256,6,64]{2,0,4,3,1:T(2,128)} dynamic-update-slice(f32[2,1,256,6,64]{2,0,4,3,1:T(2,128)} %get-tuple-element.1940, f32[1,1,256,6,64]{2,0,4,3,1:T(1,128)S(1)} %copy.365, s32[]{:T(128)} %get-tuple-element.1938, s32[]{:T(128)} %constant.179.clone.1..sunk.1, s32[]{:T(128)} %constant.179.clone.1..sunk.1, s32[]{:T(128)} %constant.179.clone.1..sunk.1, ...) | dynamic-update-slice | bytes 786436 | tf_op jit(solution)/shard_map/jvp(vmap())/while/body/jit(dynamic_update_index_in_dim)/dynamic_update_slice | solution.py:63
  56.0 2.7 multiply_dynamic-update-slice_fusion.4
  64.1 9.0 %dynamic_update_slice.218 = f32[2,1,256,6,64]{2,0,4,3,1:T(2,128)} dynamic-update-slice(f32[2,1,256,6,64]{2,0,4,3,1:T(2,128)} %get-tuple-element.1940, f32[1,1,256,6,64]{2,0,4,3,1:T(1,128)S(1)} %copy.365, s32[]{:T(128)} %get-tuple-element.1938, s32[]{:T(128)} %constant.179.clone.1..sunk.1, s32[]{:T(128)} %constant.179.clone.1..sunk.1, s32[]{:T(128)} %constant.179.clone.1..sunk.1, ...) | dynamic-update-slice | bytes 786436 | tf_op jit(solution)/shard_map/jvp(vmap())/while/body/jit(dynamic_update_index_in_dim)/dynamic_update_slice | solution.py:63
  78.1 2.1 copy.268
  80.2 2.3 copy.197
  82.7 3.4 multiply_reduce_fusion.6
  86.1 9.0 %psum.126 = f32[512]{0:T(512)} all-reduce(f32[512]{0:T(512)S(1)} %get-tuple-element.1483), channel_id=1, replica_groups=mesh['dp'=8,'tensor'=4] {'tensor'}, use_global_device_ids=true, to_apply=%region_6.7 | all-reduce | flops 512 | bytes 4096 | tf_op jit(solution)/shard_map/psum | solution.py:153
  95.9 2.8 convolution_convert_fusion
  98.7 2.1 multiply_reduce_fusion
  100.8 6.0 %psum.128 = f32[512]{0:T(512)S(1)} all-reduce(f32[512]{0:T(512)} %get-tuple-element.1335), channel_id=1, replica_groups=mesh['dp'=8,'tensor'=4] {'tensor'}, use_global_device_ids=true, to_apply=%region_9.10 | all-reduce | flops 512 | bytes 4096 | tf_op jit(solution)/shard_map/psum | solution.py:165
  106.8 4.1 fusion.156
  117.5 114.6 %while.70 = (s32[]{:T(128)}, f32[1,6,64,128]{3,2,1,0:T(8,128)S(1)}, f32[2,1,256,6,64]{2,0,4,3,1:T(2,128)}, f32[2,1,256,128]{3,2,1,0:T(8,128)}, f32[2,1,256,128]{...) while((s32[]{:T(128)}, f32[1,6,64,128]{3,2,1,0:T(8,128)S(1)}, ...), condition=%wide.region_21.22_spmd.clone, body=%wide.region_10.21_spmd.clone.sunk | while | flops 1414609920 | bytes 22201356 | solution.py:63
  120.7 4.7 fusion.270
  137.1 8.8 %reduce-window.46 = f32[1,6,2,128]{3,2,1,0:T(2,128)} reduce-window(f32[1,6,2,128]{3,2,1,0:T(2,128)} %bitcast.662, f32[]{:T(128)} %constant.180.clone.1..sunk), window={size=1x1x1x128 pad=0_0x0_0x0_0x0_127}, to_apply=%region_19.19 | reduce-window | flops 195072 | bytes 12292 | tf_op jit(solution)/shard_map/reduce-window.18
  155.8 2.5 fusion.269
  158.7 9.0 %dynamic_update_slice.208 = f32[2,1,256,6,64]{2,0,4,3,1:T(2,128)} dynamic-update-slice(f32[2,1,256,6,64]{2,0,4,3,1:T(2,128)} %get-tuple-element.2025, f32[1,1,256,6,64]{2,0,4,3,1:T(1,128)S(1)} %copy.356, s32[]{:T(128)S(6)} %sub.180, s32[]{:T(128)} %constant.179.clone.1..sunk, s32[]{:T(128)} %constant.179.clone.1..sunk, s32[]{:T(128)} %constant.179.clone.1..sunk, s32[]{:T(128)} %constant.179.clone.1..sunk) | dynamic-update-slice | bytes 786436 | tf_op jit(solution)/shard_map/transpose(jvp(vmap()))/while/body/jit(dynamic_update_index_in_dim)/dynamic_update_slice | solution.py:63
  178.0 4.7 fusion.270
  194.3 8.8 %reduce-window.46 = f32[1,6,2,128]{3,2,1,0:T(2,128)} reduce-window(f32[1,6,2,128]{3,2,1,0:T(2,128)} %bitcast.662, f32[]{:T(128)} %constant.180.clone.1..sunk), window={size=1x1x1x128 pad=0_0x0_0x0_0x0_127}, to_apply=%region_19.19 | reduce-window | flops 195072 | bytes 12292 | tf_op jit(solution)/shard_map/reduce-window.18
  213.1 2.5 fusion.269
  216.0 9.0 %dynamic_update_slice.208 = f32[2,1,256,6,64]{2,0,4,3,1:T(2,128)} dynamic-update-slice(f32[2,1,256,6,64]{2,0,4,3,1:T(2,128)} %get-tuple-element.2025, f32[1,1,256,6,64]{2,0,4,3,1:T(1,128)S(1)} %copy.356, s32[]{:T(128)S(6)} %sub.180, s32[]{:T(128)} %constant.179.clone.1..sunk, s32[]{:T(128)} %constant.179.clone.1..sunk, s32[]{:T(128)} %constant.179.clone.1..sunk, s32[]{:T(128)} %constant.179.clone.1..sunk) | dynamic-update-slice | bytes 786436 | tf_op jit(solution)/shard_map/transpose(jvp(vmap()))/while/body/jit(dynamic_update_index_in_dim)/dynamic_update_slice | solution.py:63
  226.6 2.0 fusion.272
  232.2 2.2 copy.269
  234.4 2.3 copy.212
  236.7 2.1 multiply_reduce_fusion.3
  257.0 38.6 %all-reduce.23 = (f32[768,6]{0,1:T(8,128)}, f32[4,384]{1,0:T(4,128)}, f32[384]{0:T(512)}, f32[6]{0:T(128)}, f32[6]{0:T(128)}, /*index=5*/f32[6]{0:T(128)}, f32[384]{0:T(512)}) all-reduce(f32[768,6]{0,1:T(8,128)S(1)} %fusion.173, f32[4,384]{1,0:T(4,128)S(1)} %pad_add_fusion.6, ...), channel_id=1, replica_groups=mesh['dp'=8,'tensor'=4] {'dp'}, use_global_device_ids=true, to_apply=%region_30.31 | all-reduce | flops 6930 | bytes 55440 | tf_op jit(solution)/shard_map/psum | solution.py:196
  298.1 37.1 %all-reduce.22 = (f32[768]{0:T(1024)}, f32[4,256]{1,0:T(4,128)}, f32[256]{0:T(256)}) all-reduce(f32[768]{0:T(1024)S(1)} %fusion.166, f32[4,256]{1,0:T(4,128)S(1)} %pad_add_fusion.7, f32[256]{0:T(256)S(1)} %get-tuple-element.1344), channel_id=1, replica_groups=mesh['dp'=8,'tensor'=4] {'dp','tensor'}, use_global_device_ids=true, to_apply=%region_26.27 | all-reduce | flops 2048 | bytes 16384 | tf_op jit(solution)/shard_map/psum | solution.py:193
  335.6 3.2 fusion.149
  338.7 86.3 %all-reduce.30.cloned.1.call-done = f32[768,256]{1,0:T(8,128)} async-done(((f32[768,256]{1,0:T(8,128)}), f32[768,256]{1,0:T(8,128)}) %all-reduce.30.cloned.1.call-update) | async-done | bytes 786448 | tf_op jit(solution)/shard_map/psum | solution.py:193
  425.1 142.8 %all-reduce.32.cloned.1.call-done = (f32[768,384]{1,0:T(8,128)}, f32[768,384]{1,0:T(8,128)}, f32[384,768]{1,0:T(8,128)}) async-done(((f32[768,384]{1,0:T(8,128)}, f32[768,384]{1,0:T(8,128)}, f32[384,768]{1,0:T(8,128)}), (f32[768,384]{1,0:T(8,128)}, f32[768,384]{1,0:T(8,128)}, f32[384,768]{1,0:T(8,128)})) %all-reduce.32.cloned.1.call-update) | async-done | bytes 3538960 | tf_op jit(solution)/shard_map/psum | solution.py:196
  567.9 2.5 copy.471
  (452 shorter events, 140.9 us)
Async XLA Ops:
  7.2 75.5 %copy-start = (bf16[768,384]{1,0:T(8,128)(2,1)S(1)}, bf16[768,384]{1,0:T(8,128)(2,1)}, u32[]{:S(2)}) copy-start(bf16[768,384]{1,0:T(8,128)(2,1)} %param.23) | copy-start | bytes 1769476
  7.2 288.5 %all-reduce.34.cloned.1.call-start = ((), (), s32[]{:S(2)}) async-start(), calls=%async_computation.2 | async-start | bytes 3145728 | tf_op jit(solution)/shard_map/psum | solution.py:157
  8.8 10.7 %copy-start.83 = (f32[512]{0:T(512)}, f32[512]{0:T(512)S(1)}, u32[]{:S(2)}) copy-start(f32[512]{0:T(512)S(1)} %fusion.176) | copy-start | bytes 6148
  23.5 7.8 %copy-start.28 = (f32[2,1,256,6]{2,3,1,0:T(8,128)}, f32[2,1,256,6]{2,3,1,0:T(8,128)S(1)}, u32[]{:S(2)}) copy-start(f32[2,1,256,6]{2,3,1,0:T(8,128)S(1)} %get-tuple-element.1985) | copy-start | bytes 36868 | tf_op jit(solution)/shard_map/jvp(vmap())/while
  45.8 5.0 copy-start.29
  50.7 7.9 %copy-start.28 = (f32[2,1,256,6]{2,3,1,0:T(8,128)}, f32[2,1,256,6]{2,3,1,0:T(8,128)S(1)}, u32[]{:S(2)}) copy-start(f32[2,1,256,6]{2,3,1,0:T(8,128)S(1)} %get-tuple-element.1985) | copy-start | bytes 36868 | tf_op jit(solution)/shard_map/jvp(vmap())/while
  73.1 5.0 copy-start.29
  78.1 4.6 copy-start.69
  78.1 4.6 copy-start.84
  82.7 24.1 %copy-start.56 = (f32[384]{0:T(512)}, f32[384]{0:T(512)S(1)}, u32[]{:S(2)}) copy-start(f32[384]{0:T(512)S(1)} %mul.847) | copy-start | bytes 4612
  82.7 13.2 %copy-start.54 = (f32[384]{0:T(512)S(1)}, f32[384]{0:T(512)}, u32[]{:S(2)}) copy-start(f32[384]{0:T(512)} %param.34) | copy-start | bytes 4612
  86.1 12.6 %copy-start.3 = (f32[512,384]{1,0:T(8,128)S(1)}, f32[512,384]{1,0:T(8,128)}, u32[]{:S(2)}) copy-start(f32[512,384]{1,0:T(8,128)} %get-tuple-element.1484) | copy-start | bytes 2359300
  86.1 12.6 %copy-start.15 = (bf16[384,768]{1,0:T(8,128)(2,1)S(1)}, bf16[384,768]{1,0:T(8,128)(2,1)}, u32[]{:S(2)}) copy-start(bf16[384,768]{1,0:T(8,128)(2,1)} %param.35) | copy-start | bytes 1769476
  95.9 11.0 %copy-start.49 = (f32[512]{0:T(512)}, f32[512]{0:T(512)S(1)}, u32[]{:S(2)}) copy-start(f32[512]{0:T(512)S(1)} %get-tuple-element.1530) | copy-start | bytes 6148
  112.3 5.1 copy-start.7
  117.5 7.9 %copy-start.16 = (pred[256,256]{1,0:T(8,128)(4,1)}, pred[256,256]{1,0:T(8,128)(4,1)S(1)}, u32[]{:S(2)}) copy-start(pred[256,256]{1,0:T(8,128)(4,1)S(1)} %get-tuple-element.2081) | copy-start | bytes 196612 | tf_op jit(solution)/shard_map/transpose(jvp(vmap()))/while
  167.7 5.5 copy-start.14
  167.7 5.5 copy-start.24
  167.7 6.4 %copy-start.96 = (f32[2,1,6,1,1]{2,4,3,1,0:T(1,128)S(1)}, f32[2,1,6,1,1]{2,4,3,1,0:T(1,128)}, u32[]{:S(2)}) copy-start(f32[2,1,6,1,1]{2,4,3,1,0:T(1,128)} %get-tuple-element.2061) | copy-start | bytes 148 | tf_op jit(solution)/shard_map/transpose(jvp(vmap()))/while
  169.3 5.5 copy-start.17
  174.8 7.9 %copy-start.16 = (pred[256,256]{1,0:T(8,128)(4,1)}, pred[256,256]{1,0:T(8,128)(4,1)S(1)}, u32[]{:S(2)}) copy-start(pred[256,256]{1,0:T(8,128)(4,1)S(1)} %get-tuple-element.2081) | copy-start | bytes 196612 | tf_op jit(solution)/shard_map/transpose(jvp(vmap()))/while
  224.9 5.5 copy-start.14
  224.9 5.5 copy-start.24
  224.9 6.4 %copy-start.96 = (f32[2,1,6,1,1]{2,4,3,1,0:T(1,128)S(1)}, f32[2,1,6,1,1]{2,4,3,1,0:T(1,128)}, u32[]{:S(2)}) copy-start(f32[2,1,6,1,1]{2,4,3,1,0:T(1,128)} %get-tuple-element.2061) | copy-start | bytes 148 | tf_op jit(solution)/shard_map/transpose(jvp(vmap()))/while
  226.5 5.5 copy-start.17
  232.2 4.5 copy-start.6
  232.2 4.5 copy-start.13
  232.2 4.5 copy-start.57
  246.3 178.8 %all-reduce.30.cloned.1.call-start = ((), (), s32[]{:S(2)}) async-start(), calls=%async_computation | async-start | bytes 1572864 | tf_op jit(solution)/shard_map/psum | solution.py:193
  248.8 319.1 %all-reduce.32.cloned.1.call-start = ((), (), s32[]{:S(2)}) async-start(), calls=%async_computation.1 | async-start | bytes 7077888 | tf_op jit(solution)/shard_map/psum | solution.py:196
  295.7 39.6 %copy-start.10 = (bf16[512,768]{1,0:T(8,128)(2,1)S(1)}, bf16[512,768]{1,0:T(8,128)(2,1)}, u32[]{:S(2)}) copy-start(bf16[512,768]{1,0:T(8,128)(2,1)} %get-tuple-element.1468) | copy-start | bytes 2359300
  297.0 38.6 %copy-start.59 = (f32[512]{0:T(512)S(1)}, f32[512]{0:T(512)}, u32[]{:S(2)}) copy-start(f32[512]{0:T(512)} %copy-done.58) | copy-start | bytes 6148
  (93 other events, 194.0 us)
Sparse Core Ops, SparseCore 0:
  246.4 43.3 all-reduce.33
  295.0 130.0 all-reduce.29
  430.1 137.7 all-reduce.31
where the time goes:
time: 585 us; the launch traced here: 580 us
  waiting for transfers between devices  229 us (39%)
  local copies, waits for them, and re-layouts  118 us (20%)
  blocking collectives  90.8 us (16%)
  other arithmetic  71.2 us (12%)
  matrix products  55.8 us (10%)
  between operations  14.7 us (3%)
    psum x1, waiting for transfers between devices, per_device(): lax.psum((grad_w_z, grad_w_x, grad_w_dt, back[3], back[4], back[7], back[...  143 us
    psum x1, waiting for transfers between devices, per_device(): lax.psum((grad_w_bc, back[5], back[6], grad_norm_gain), ('dp', 'tensor'))  86.3 us
    dynamic_update_slice x26, local copies, waits for them, and re-layouts, state_scan(): _, outputs = lax.scan(advance, initial, pieces)  44.2 us
    psum x1, blocking collectives, per_device(): lax.psum((grad_w_z, grad_w_x, grad_w_dt, back[3], back[4], back[7], back[...  38.6 us
    psum x1, blocking collectives, per_device(): lax.psum((grad_w_bc, back[5], back[6], grad_norm_gain), ('dp', 'tensor'))  37.1 us
    another operation x19, other arithmetic  26.7 us
    another operation x28, local copies, waits for them, and re-layouts  18.7 us
    dot_general x6, matrix products, advance(): inside = jnp.einsum('tsh,shp->thp', mixing, x_blk, precision=highest)  18.1 us
  transfers between devices with their start and end apart: 3, of which 2 were waited for; matrix products, arithmetic and copies ran while one was open for 3% of the time, Pallas kernels for 0%

commit v1 on v0

--- a/solution.py
+++ b/solution.py
@@ -191,7 +191,7 @@
     grad_x = (cotan.astype(jnp.float32) + d_tokens).astype(jnp.bfloat16)
     grad_x = grad_x.reshape(seq_count, length, width)
     grad_w_bc, grad_conv_bc, grad_conv_bc_bias, grad_norm_gain = lax.psum(
-        (grad_w_bc, back[5], back[6], grad_norm_gain), ("dp", "tensor")
+        lax.psum((grad_w_bc, back[5], back[6], grad_norm_gain), "tensor"), "dp"
     )
     reduced = lax.psum(
         (

time: 585 us -> 462 us (0.79)
  waiting for transfers between devices: 229 us -> 170 us
  blocking collectives: 90.8 us -> 61.8 us
  local copies, waits for them, and re-layouts: 118 us -> 94.1 us
  other arithmetic: 71.2 us -> 55.8 us
    psum x1, waiting for transfers between devices: 86.3 us -> 14.4 us  [per_device(): lax.psum((grad_w_bc, back[5], back[6], grad_norm_gain), 'tensor')]
    psum x1, waiting for transfers between devices: 0.02 us -> 42.8 us  [per_device(): lax.psum(partial_out.astype(jnp.bfloat16), 'tensor').astype(jnp.float32)]
    psum x1, waiting for transfers between devices: 143 us -> 113 us  [per_device(): lax.psum((grad_w_z, grad_w_x, grad_w_dt, back[3], back[4], back[7], back[...]
    psum x2, blocking collectives: 75.7 us -> 47.4 us  [the longest x1 41.3 us: per_device(): lax.psum(lax.psum((grad_w_bc, back[5], back[6], grad_norm_gain), 'tensor'...]
    another operation x28, local copies, waits for them, and re-layouts: 18.7 us -> 7.29 us
    another operation x19, other arithmetic: 26.7 us -> 19.1 us
    unnamed x152 -> x138, local copies, waits for them, and re-layouts: 16 us -> 15.6 us
  transfers between devices with their start and end apart: 3 -> 3, of which waited for: 2 -> 3; matrix products, arithmetic and copies ran while one was open for 3% -> 6% of each run, Pallas kernels for 0% -> 0%
where the time goes in v1:
time: 462 us; the launch traced here: 458 us
  waiting for transfers between devices  170 us (37%)
  local copies, waits for them, and re-layouts  94.1 us (20%)
  blocking collectives  61.8 us (13%)
  matrix products  60 us (13%)
  other arithmetic  55.8 us (12%)
  between operations  14.6 us (3%)
    psum x1, waiting for transfers between devices, per_device(): lax.psum((grad_w_z, grad_w_x, grad_w_dt, back[3], back[4], back[7], back[...  113 us
    dynamic_update_slice x26, local copies, waits for them, and re-layouts, state_scan(): _, outputs = lax.scan(advance, initial, pieces)  43 us
    psum x1, waiting for transfers between devices, per_device(): lax.psum(partial_out.astype(jnp.bfloat16), 'tensor').astype(jnp.float32)  42.8 us
    psum x1, blocking collectives, per_device(): lax.psum(lax.psum((grad_w_bc, back[5], back[6], grad_norm_gain), 'tensor'...  41.3 us
    another operation x19, other arithmetic  19.1 us
    dot_general x6, matrix products, advance(): inside = jnp.einsum('tsh,shp->thp', mixing, x_blk, precision=highest)  16.8 us
    unnamed x138, local copies, waits for them, and re-layouts  15.6 us
    psum x1, waiting for transfers between devices, per_device(): lax.psum((grad_w_bc, back[5], back[6], grad_norm_gain), 'tensor')  14.4 us
  transfers between devices with their start and end apart: 3, of which 3 were waited for; matrix products, arithmetic and copies ran while one was open for 6% of the time, Pallas kernels for 0%

profile of v1, /device:TPU:0, one launch (start us, length us, event | category | flops | bytes accessed | tf_op | source)
XLA Modules:
  0.0 457.5 jit_solution(2325202235306323347)
XLA Ops:
  23.4 56.0 %while.71 = (s32[]{:T(128)}, f32[1,6,64,128]{3,2,1,0:T(8,128)S(1)}, f32[2,1,256,6,64]{2,0,4,3,1:T(2,128)}, f32[2,1,128,256]{2,3,1,0:T(8,128)}, f32[2,1,256,256,6...) while((s32[]{:T(128)}, f32[1,6,64,128]{3,2,1,0:T(8,128)S(1)}, ...), condition=%wide.region_4.5_spmd.clone.clone, body=%wide.region_1.4_spmd.clone.clone.sunk | while | flops 708627456 | bytes 15232577 | solution.py:63
  29.4 2.6 multiply_dynamic-update-slice_fusion.4
  37.4 9.0 %dynamic_update_slice.218 = f32[2,1,256,6,64]{2,0,4,3,1:T(2,128)} dynamic-update-slice(f32[2,1,256,6,64]{2,0,4,3,1:T(2,128)} %get-tuple-element.1944, f32[1,1,256,6,64]{2,0,4,3,1:T(1,128)S(1)} %copy.365, s32[]{:T(128)} %get-tuple-element.1942, s32[]{:T(128)} %constant.179.clone.1..sunk.1, s32[]{:T(128)} %constant.179.clone.1..sunk.1, s32[]{:T(128)} %constant.179.clone.1..sunk.1, ...) | dynamic-update-slice | bytes 786436 | tf_op jit(solution)/shard_map/jvp(vmap())/while/body/jit(dynamic_update_index_in_dim)/dynamic_update_slice | solution.py:63
  57.3 2.7 multiply_dynamic-update-slice_fusion.4
  65.5 9.0 %dynamic_update_slice.218 = f32[2,1,256,6,64]{2,0,4,3,1:T(2,128)} dynamic-update-slice(f32[2,1,256,6,64]{2,0,4,3,1:T(2,128)} %get-tuple-element.1944, f32[1,1,256,6,64]{2,0,4,3,1:T(1,128)S(1)} %copy.365, s32[]{:T(128)} %get-tuple-element.1942, s32[]{:T(128)} %constant.179.clone.1..sunk.1, s32[]{:T(128)} %constant.179.clone.1..sunk.1, s32[]{:T(128)} %constant.179.clone.1..sunk.1, ...) | dynamic-update-slice | bytes 786436 | tf_op jit(solution)/shard_map/jvp(vmap())/while/body/jit(dynamic_update_index_in_dim)/dynamic_update_slice | solution.py:63
  79.5 2.1 copy.268
  81.6 2.3 copy.197
  84.0 3.4 multiply_reduce_fusion.6
  87.4 8.5 %psum.154 = f32[512]{0:T(512)S(1)} all-reduce(f32[512]{0:T(512)S(1)} %get-tuple-element.1487), channel_id=1, replica_groups=mesh['dp'=8,'tensor'=4] {'tensor'}, use_global_device_ids=true, to_apply=%region_6.7 | all-reduce | flops 512 | bytes 4096 | tf_op jit(solution)/shard_map/psum | solution.py:153
  95.9 3.6 multiply_reduce_fusion
  99.5 5.9 %psum.156 = f32[512]{0:T(512)S(1)} all-reduce(f32[512]{0:T(512)S(1)} %get-tuple-element.1335), channel_id=1, replica_groups=mesh['dp'=8,'tensor'=4] {'tensor'}, use_global_device_ids=true, to_apply=%region_9.10 | all-reduce | flops 512 | bytes 4096 | tf_op jit(solution)/shard_map/psum | solution.py:165
  105.5 4.2 fusion.156
  116.1 76.4 %while.70 = (s32[]{:T(128)}, f32[1,6,64,128]{3,2,1,0:T(8,128)S(1)}, f32[2,1,256,6,64]{2,0,4,3,1:T(2,128)}, f32[2,1,256,128]{3,2,1,0:T(8,128)}, f32[2,1,256,128]{...) while((s32[]{:T(128)}, f32[1,6,64,128]{3,2,1,0:T(8,128)S(1)}, ...), condition=%wide.region_21.22_spmd.clone, body=%wide.region_10.21_spmd.clone.sunk | while | flops 1414609920 | bytes 19924064 | solution.py:63
  119.4 4.0 fusion.270
  127.9 7.6 %reduce-window.46 = f32[1,6,2,128]{3,2,1,0:T(2,128)S(1)} reduce-window(f32[1,6,2,128]{3,2,1,0:T(2,128)S(1)} %bitcast.662, f32[]{:T(128)} %constant.180.clone.1..sunk), window={size=1x1x1x128 pad=0_0x0_0x0_0x0_127}, to_apply=%region_19.19 | reduce-window | flops 195072 | bytes 12292 | tf_op jit(solution)/shard_map/reduce-window.18
  135.9 2.5 fusion.269
  138.8 9.0 %dynamic_update_slice.208 = f32[2,1,256,6,64]{2,0,4,3,1:T(2,128)} dynamic-update-slice(f32[2,1,256,6,64]{2,0,4,3,1:T(2,128)} %get-tuple-element.2029, f32[1,1,256,6,64]{2,0,4,3,1:T(1,128)S(1)} %copy.356, s32[]{:T(128)S(6)} %sub.180, s32[]{:T(128)} %constant.179.clone.1..sunk, s32[]{:T(128)} %constant.179.clone.1..sunk, s32[]{:T(128)} %constant.179.clone.1..sunk, s32[]{:T(128)} %constant.179.clone.1..sunk) | dynamic-update-slice | bytes 786436 | tf_op jit(solution)/shard_map/transpose(jvp(vmap()))/while/body/jit(dynamic_update_index_in_dim)/dynamic_update_slice | solution.py:63
  149.6 1.9 fusion.272
  157.5 4.0 fusion.270
  166.0 7.6 %reduce-window.46 = f32[1,6,2,128]{3,2,1,0:T(2,128)S(1)} reduce-window(f32[1,6,2,128]{3,2,1,0:T(2,128)S(1)} %bitcast.662, f32[]{:T(128)} %constant.180.clone.1..sunk), window={size=1x1x1x128 pad=0_0x0_0x0_0x0_127}, to_apply=%region_19.19 | reduce-window | flops 195072 | bytes 12292 | tf_op jit(solution)/shard_map/reduce-window.18
  174.0 2.5 fusion.269
  176.9 9.0 %dynamic_update_slice.208 = f32[2,1,256,6,64]{2,0,4,3,1:T(2,128)} dynamic-update-slice(f32[2,1,256,6,64]{2,0,4,3,1:T(2,128)} %get-tuple-element.2029, f32[1,1,256,6,64]{2,0,4,3,1:T(1,128)S(1)} %copy.356, s32[]{:T(128)S(6)} %sub.180, s32[]{:T(128)} %constant.179.clone.1..sunk, s32[]{:T(128)} %constant.179.clone.1..sunk, s32[]{:T(128)} %constant.179.clone.1..sunk, s32[]{:T(128)} %constant.179.clone.1..sunk) | dynamic-update-slice | bytes 786436 | tf_op jit(solution)/shard_map/transpose(jvp(vmap()))/while/body/jit(dynamic_update_index_in_dim)/dynamic_update_slice | solution.py:63
  192.6 2.6 multiply_reduce_fusion.9
  198.0 2.6 fusion.202
  203.1 2.3 copy.212
  205.4 2.3 multiply_reduce_fusion.3
  219.2 14.4 %all-reduce.30.cloned.1.call-done = f32[768,256]{1,0:T(8,128)} async-done(((f32[768,256]{1,0:T(8,128)}), f32[768,256]{1,0:T(8,128)}) %all-reduce.30.cloned.1.call-update) | async-done | bytes 786448 | tf_op jit(solution)/shard_map/psum | solution.py:194
  236.7 42.8 %all-reduce.34.cloned.1.call-done = (bf16[512,768]{1,0:T(8,128)(2,1)}, bf16[512,768]{1,0:T(8,128)(2,1)}) async-done(((bf16[512,768]{1,0:T(8,128)(2,1)}, bf16[512,768]{1,0:T(8,128)(2,1)}), (bf16[512,768]{1,0:T(8,128)(2,1)}, bf16[512,768]{1,0:T(8,128)(2,1)})) %all-reduce.34.cloned.1.call-update) | async-done | bytes 1572880 | tf_op jit(solution)/shard_map/psum | solution.py:157
  281.9 6.0 %all-reduce.24 = (f32[768]{0:T(1024)S(1)}, f32[4,256]{1,0:T(4,128)S(1)}, f32[256]{0:T(256)S(1)}) all-reduce(f32[768]{0:T(1024)S(1)} %fusion.166, f32[4,256]{1,0:T(4,128)S(1)} %pad_add_fusion.7, f32[256]{0:T(256)S(1)} %get-tuple-element.1344), channel_id=1, replica_groups=mesh['dp'=8,'tensor'=4] {'tensor'}, use_global_device_ids=true, to_apply=%region_26.27 | all-reduce | flops 2048 | bytes 16384 | tf_op jit(solution)/shard_map/psum | solution.py:194
  287.9 41.3 %all-reduce.22 = (f32[768]{0:T(1024)}, f32[768,6]{0,1:T(8,128)}, f32[4,384]{1,0:T(4,128)}, f32[384]{0:T(512)}, f32[4,256]{1,0:T(4,128)}, /*index=5*/f32[256]{0:T...) all-reduce(f32[768]{0:T(1024)S(1)} %get-tuple-element.1468, ...), channel_id=1, replica_groups=mesh['dp'=8,'tensor'=4] {'dp'}, use_global_device_ids=true, to_apply=%region_27.28 | all-reduce | flops 8978 | bytes 71824 | tf_op jit(solution)/shard_map/psum | solution.py:193
  332.2 112.9 %all-reduce.32.cloned.1.call-done = (f32[768,384]{1,0:T(8,128)}, f32[768,384]{1,0:T(8,128)}, f32[768,256]{1,0:T(8,128)}, f32[384,768]{1,0:T(8,128)}) async-done(((f32[768,384]{1,0:T(8,128)}, f32[768,384]{1,0:T(8,128)}, f32[768,256]{1,0:T(8,128)}, f32[384,768]{1,0:T(8,128)}), (f32[768,384]{1,0:T(8,128)}, f32[768,384]{1,0:T(8,128)}, f32[768,256]{1,0:T(8,128)}, ...) | async-done | bytes 4325392 | tf_op jit(solution)/shard_map/psum | solution.py:196
  445.1 2.5 copy.472
  (442 shorter events, 111.1 us)
Async XLA Ops:
  7.2 76.8 %copy-start = (bf16[768,384]{1,0:T(8,128)(2,1)S(1)}, bf16[768,384]{1,0:T(8,128)(2,1)}, u32[]{:S(2)}) copy-start(bf16[768,384]{1,0:T(8,128)(2,1)} %param.23) | copy-start | bytes 1769476
  7.2 226.4 %all-reduce.30.cloned.1.call-start = ((), (), s32[]{:S(2)}) async-start(), calls=%async_computation | async-start | bytes 1572864 | tf_op jit(solution)/shard_map/psum | solution.py:194
  8.8 10.7 %copy-start.77 = (f32[512]{0:T(512)}, f32[512]{0:T(512)S(1)}, u32[]{:S(2)}) copy-start(f32[512]{0:T(512)S(1)} %fusion.176) | copy-start | bytes 6148
  46.4 4.2 copy-start.26
  46.4 4.3 copy-start.14
  74.5 4.2 copy-start.26
  74.5 4.2 copy-start.14
  79.5 4.4 copy-start.86
  79.5 4.5 copy-start.63
  79.5 4.5 copy-start.78
  84.0 21.4 %copy-start.50 = (f32[384]{0:T(512)}, f32[384]{0:T(512)S(1)}, u32[]{:S(2)}) copy-start(f32[384]{0:T(512)S(1)} %mul.847) | copy-start | bytes 4612
  84.0 11.9 %copy-start.49 = (f32[384]{0:T(512)S(1)}, f32[384]{0:T(512)}, u32[]{:S(2)}) copy-start(f32[384]{0:T(512)} %param.34) | copy-start | bytes 4612
  87.4 18.1 %copy-start.3 = (f32[512,384]{1,0:T(8,128)S(1)}, f32[512,384]{1,0:T(8,128)}, u32[]{:S(2)}) copy-start(f32[512,384]{1,0:T(8,128)} %get-tuple-element.1488) | copy-start | bytes 2359300
  119.4 5.2 %copy-start.21 = (f32[2,1,256,6]{2,3,1,0:T(8,128)S(1)}, f32[2,1,256,6]{2,3,1,0:T(8,128)}, u32[]{:S(2)}) copy-start(f32[2,1,256,6]{2,3,1,0:T(8,128)} %get-tuple-element.2081) | copy-start | bytes 36868 | tf_op jit(solution)/shard_map/transpose(jvp(vmap()))/while
  123.3 12.4 %copy-start.44 = (f32[2,1,256,6]{2,0,3,1:T(2,128)S(1)}, f32[2,1,256,6]{2,0,3,1:T(2,128)}, u32[]{:S(2)}) copy-start(f32[2,1,256,6]{2,0,3,1:T(2,128)} %get-tuple-element.2033) | copy-start | bytes 36868 | tf_op jit(solution)/shard_map/transpose(jvp(vmap()))/while
  123.3 12.5 %copy-start.36 = (f32[2,1,256,6,1]{2,0,4,3,1:T(2,128)S(1)}, f32[2,1,256,6,1]{2,0,4,3,1:T(2,128)}, u32[]{:S(2)}) copy-start(f32[2,1,256,6,1]{2,0,4,3,1:T(2,128)} %get-tuple-element.2070) | copy-start | bytes 36868 | tf_op jit(solution)/shard_map/transpose(jvp(vmap()))/while
  123.3 12.5 %copy-start.39 = (f32[2,1,256,6,1]{2,0,4,3,1:T(2,128)S(1)}, f32[2,1,256,6,1]{2,0,4,3,1:T(2,128)}, u32[]{:S(2)}) copy-start(f32[2,1,256,6,1]{2,0,4,3,1:T(2,128)} %get-tuple-element.2067) | copy-start | bytes 36868 | tf_op jit(solution)/shard_map/transpose(jvp(vmap()))/while
  138.4 13.2 %copy-start.40 = (f32[2,1,256,6]{2,3,1,0:T(8,128)S(1)}, f32[2,1,256,6]{2,3,1,0:T(8,128)}, u32[]{:S(2)}) copy-start(f32[2,1,256,6]{2,3,1,0:T(8,128)} %get-tuple-element.2032) | copy-start | bytes 36868 | tf_op jit(solution)/shard_map/transpose(jvp(vmap()))/while
  147.8 4.4 copy-start.11
  147.8 5.9 %copy-start.90 = (f32[2,1,6,1,1]{2,4,3,1,0:T(1,128)S(1)}, f32[2,1,6,1,1]{2,4,3,1,0:T(1,128)}, u32[]{:S(2)}) copy-start(f32[2,1,6,1,1]{2,4,3,1,0:T(1,128)} %get-tuple-element.2065) | copy-start | bytes 148 | tf_op jit(solution)/shard_map/transpose(jvp(vmap()))/while
  157.5 5.2 %copy-start.21 = (f32[2,1,256,6]{2,3,1,0:T(8,128)S(1)}, f32[2,1,256,6]{2,3,1,0:T(8,128)}, u32[]{:S(2)}) copy-start(f32[2,1,256,6]{2,3,1,0:T(8,128)} %get-tuple-element.2081) | copy-start | bytes 36868 | tf_op jit(solution)/shard_map/transpose(jvp(vmap()))/while
  161.4 12.4 %copy-start.44 = (f32[2,1,256,6]{2,0,3,1:T(2,128)S(1)}, f32[2,1,256,6]{2,0,3,1:T(2,128)}, u32[]{:S(2)}) copy-start(f32[2,1,256,6]{2,0,3,1:T(2,128)} %get-tuple-element.2033) | copy-start | bytes 36868 | tf_op jit(solution)/shard_map/transpose(jvp(vmap()))/while
  161.4 12.5 %copy-start.36 = (f32[2,1,256,6,1]{2,0,4,3,1:T(2,128)S(1)}, f32[2,1,256,6,1]{2,0,4,3,1:T(2,128)}, u32[]{:S(2)}) copy-start(f32[2,1,256,6,1]{2,0,4,3,1:T(2,128)} %get-tuple-element.2070) | copy-start | bytes 36868 | tf_op jit(solution)/shard_map/transpose(jvp(vmap()))/while
  161.4 12.5 %copy-start.39 = (f32[2,1,256,6,1]{2,0,4,3,1:T(2,128)S(1)}, f32[2,1,256,6,1]{2,0,4,3,1:T(2,128)}, u32[]{:S(2)}) copy-start(f32[2,1,256,6,1]{2,0,4,3,1:T(2,128)} %get-tuple-element.2067) | copy-start | bytes 36868 | tf_op jit(solution)/shard_map/transpose(jvp(vmap()))/while
  176.5 13.2 %copy-start.40 = (f32[2,1,256,6]{2,3,1,0:T(8,128)S(1)}, f32[2,1,256,6]{2,3,1,0:T(8,128)}, u32[]{:S(2)}) copy-start(f32[2,1,256,6]{2,3,1,0:T(8,128)} %get-tuple-element.2032) | copy-start | bytes 36868 | tf_op jit(solution)/shard_map/transpose(jvp(vmap()))/while
  185.9 4.4 copy-start.11
  185.9 5.9 %copy-start.90 = (f32[2,1,6,1,1]{2,4,3,1,0:T(1,128)S(1)}, f32[2,1,6,1,1]{2,4,3,1,0:T(1,128)}, u32[]{:S(2)}) copy-start(f32[2,1,6,1,1]{2,4,3,1,0:T(1,128)} %get-tuple-element.2065) | copy-start | bytes 148 | tf_op jit(solution)/shard_map/transpose(jvp(vmap()))/while
  197.9 81.5 %all-reduce.34.cloned.1.call-start = ((), (), s32[]{:S(2)}) async-start(), calls=%async_computation.2 | async-start | bytes 3145728 | tf_op jit(solution)/shard_map/psum | solution.py:157
  213.2 231.9 %all-reduce.32.cloned.1.call-start = ((), (), s32[]{:S(2)}) async-start(), calls=%async_computation.1 | async-start | bytes 8650752 | tf_op jit(solution)/shard_map/psum | solution.py:196
  279.4 8.5 %copy-start.80 = (f32[384]{0:T(512)S(1)}, f32[384]{0:T(512)}, u32[]{:S(2)}) copy-start(f32[384]{0:T(512)} %get-tuple-element.1334) | copy-start | bytes 4612
  279.4 49.8 %copy-start.8 = (bf16[512,768]{1,0:T(8,128)(2,1)S(1)}, bf16[512,768]{1,0:T(8,128)(2,1)}, u32[]{:S(2)}) copy-start(bf16[512,768]{1,0:T(8,128)(2,1)} %get-tuple-element.1472) | copy-start | bytes 2359300
  280.8 48.9 %copy-start.53 = (f32[512]{0:T(512)S(1)}, f32[512]{0:T(512)}, u32[]{:S(2)}) copy-start(f32[512]{0:T(512)} %copy-done.52) | copy-start | bytes 6148
  (88 other events, 182.9 us)
Sparse Core Ops, SparseCore 0:
  198.1 35.4 all-reduce.29
  236.5 42.8 all-reduce.33
  284.5 160.5 all-reduce.31
